TPU v7x, 32 devices: a whole 2x2x4 slice. The times are simulated.
32 devices in a mesh: gx: 4 (over y, core), gy: 8 (over z, x).
Axes of the slice: x: 2, y: 2, z: 4, core: 2. Of those that a mesh axis runs over, the one named last changes fastest.
Arguments:
- hidden: bfloat16 [256, 8192], P('gx', 'gy'), may hold values from -12 to 12
- lengths: int32 [256], P('gy'), may hold values from 1 to 384
- draft_ids: int32 [256], P('gy'), may hold values from 0 to 31999
- attn_gain: bfloat16 [8192], P('gy'), may hold values from 0.099609375 to 1.8984375
- w_query: bfloat16 [8192, 8192], P('gy', 'gx'), may hold values from -0.0625 to 0.0625
- w_key: bfloat16 [8192, 1024], P('gy', 'gx'), may hold values from -0.0625 to 0.0625
- w_value: bfloat16 [8192, 1024], P('gy', 'gx'), may hold values from -0.0625 to 0.0625
- w_out: bfloat16 [8192, 8192], P('gx', 'gy'), may hold values from -0.0625 to 0.0625
- cache_k: bfloat16 [256, 8, 384, 128], P('gy', 'gx'), may hold values from -240 to 240
- cache_v: bfloat16 [256, 8, 384, 128], P('gy', 'gx'), may hold values from -6 to 6
- mlp_gain: bfloat16 [8192], P('gy'), may hold values from 0.099609375 to 1.8984375
- w_gate: bfloat16 [8192, 28672], P('gy', 'gx'), may hold values from -0.0625 to 0.0625
- w_up: bfloat16 [8192, 28672], P('gy', 'gx'), may hold values from -0.0625 to 0.0625
- w_down: bfloat16 [28672, 8192], P('gx', 'gy'), may hold values from -0.03125 to 0.03125
- final_gain: bfloat16 [8192], P('gy'), may hold values from 0.099609375 to 1.8984375
- w_head: bfloat16 [8192, 32000], P('gy', 'gx'), may hold values from -1 to 1
Outputs:
- log_probs: float32 [256, 32000], P('gy', 'gx')
- draft_logprob: float32 [256], P('gy')
All inputs are finite; a program needn't handle non-finite values.
Results may differ from a plain program's by a relative error of at most 0.002.
Values may be sent and summed in bfloat16 or wider, within the bound.
No kernel may reach another device: no remote copies, remote signals or barrier semaphores. Data moves between devices by JAX's collectives and lax.ppermute only.
A program may use at most 192 MiB of HBM per device.

v0:
```python
import jax
import jax.numpy as jnp
from jax import lax
from jax.sharding import PartitionSpec as P

D = 8192
HEAD_DIM = 128
epsilon = 1e-05


def combined_all(x, axis, combine):
    everything = jax.tree.map(lambda part: lax.all_gather(part, axis), x)
    initial = jax.tree.map(lambda part: part[0], everything)

    def step(k, so_far):
        return combine(so_far, jax.tree.map(lambda part: part[k], everything))

    return lax.fori_loop(1, lax.axis_size(axis), step, initial)


def rotate(vectors, position):
    half_dim = vectors.shape[-1] // 2
    frequency = jnp.exp(
        -jnp.log(10000.0) * jnp.arange(half_dim, dtype=jnp.float32) * (2.0 / vectors.shape[-1])
    )
    angle_table = position[:, None, None] * frequency
    cosine = jnp.cos(angle_table)
    sine_part = jnp.sin(angle_table)
    first_half = vectors[..., :half_dim]
    second_half = vectors[..., half_dim:]
    return jnp.concatenate(
        [
            first_half * cosine - second_half * sine_part,
            second_half * cosine + first_half * sine_part,
        ],
        axis=-1,
    )


def normalize_rows(activity, gain_row):
    squares = lax.psum(jnp.sum(activity * activity, axis=1), "gy")
    factor = lax.rsqrt(squares / D + epsilon)
    normed = (activity * factor[:, None] * gain_row.astype(jnp.float32)).astype(jnp.bfloat16)
    return lax.all_gather(normed, "gx", axis=0, tiled=True)


def attend_one(queries, own_key, own_value, cached_keys, values, usable):
    scaling = queries.shape[-1] ** (-0.5)
    scores = (
        jnp.einsum("bgd,btd->bgt", queries, cached_keys, preferred_element_type=jnp.float32)
        * scaling
    )
    own_score = (
        jnp.einsum("bgd,bd->bg", queries, own_key, preferred_element_type=jnp.float32) * scaling
    )
    scores = jnp.where(usable[:, None, :], scores, -jnp.inf)
    highest = jnp.maximum(jnp.max(scores, axis=2), own_score)
    weights = jnp.exp(scores - highest[:, :, None])
    own_weight = jnp.exp(own_score - highest)
    denominator = jnp.sum(weights, axis=2) + own_weight
    weights = (weights / denominator[:, :, None]).astype(jnp.bfloat16)
    own_weight = (own_weight / denominator).astype(jnp.bfloat16)
    blended = jnp.einsum("bgt,btd->bgd", weights, values, preferred_element_type=jnp.float32)
    blended = (
        blended
        + own_weight.astype(jnp.float32)[:, :, None] * own_value.astype(jnp.float32)[:, None, :]
    )
    return blended.astype(jnp.bfloat16)


def combine_totals(former, latter):
    highest = jnp.maximum(former[0], latter[0])
    summed = former[1] * jnp.exp(former[0] - highest) + latter[1] * jnp.exp(latter[0] - highest)
    return (highest, summed, former[2] + latter[2])


def shards(
    hidden,
    lengths,
    draft_ids,
    attn_gain,
    w_query,
    w_key,
    w_value,
    w_out,
    cache_k,
    cache_v,
    mlp_gain,
    w_gate,
    w_up,
    w_down,
    final_gain,
    w_head,
):
    residual = hidden.astype(jnp.float32)
    tokens = normalize_rows(residual, attn_gain)
    row_slab = tokens
    projected = lax.psum_scatter(
        jnp.concatenate(
            [
                jnp.dot(row_slab, w_query, preferred_element_type=jnp.float32),
                jnp.dot(row_slab, w_key, preferred_element_type=jnp.float32),
                jnp.dot(row_slab, w_value, preferred_element_type=jnp.float32),
            ],
            axis=1,
        ),
        "gy",
        scatter_dimension=0,
        tiled=True,
    )
    query_width = w_query.shape[1]
    key_width = w_key.shape[1]
    local_rows = projected.shape[0]
    position = lengths.astype(jnp.float32)
    queries = rotate(projected[:, :query_width].reshape(local_rows, -1, HEAD_DIM), position).astype(
        jnp.bfloat16
    )
    new_keys = rotate(
        projected[:, query_width : query_width + key_width].reshape(local_rows, -1, HEAD_DIM),
        position,
    ).astype(jnp.bfloat16)
    new_values = (
        projected[:, query_width + key_width :]
        .reshape(local_rows, -1, HEAD_DIM)
        .astype(jnp.bfloat16)
    )
    local_heads = new_keys.shape[1]
    queries = queries.reshape(local_rows, local_heads, -1, HEAD_DIM)
    usable = jnp.arange(cache_k.shape[2], dtype=jnp.int32)[None, :] < lengths[:, None]
    attended = jax.vmap(attend_one, in_axes=(1, 1, 1, 1, 1, None), out_axes=1)(
        queries, new_keys, new_values, cache_k, cache_v, usable
    )
    attended = attended.reshape(local_rows, query_width)
    all_heads = lax.all_gather(attended, "gy", axis=0, tiled=True)
    row_slab = all_heads
    attention_output = lax.psum_scatter(
        jnp.dot(row_slab, w_out, preferred_element_type=jnp.float32),
        "gx",
        scatter_dimension=0,
        tiled=True,
    )
    after_attention = (residual + attention_output).astype(jnp.bfloat16)
    mlp_tokens = normalize_rows(after_attention.astype(jnp.float32), mlp_gain)
    hidden_width = w_gate.shape[1]
    row_slab = mlp_tokens
    summed = lax.psum_scatter(
        jnp.concatenate(
            [
                jnp.dot(row_slab, w_gate, preferred_element_type=jnp.float32),
                jnp.dot(row_slab, w_up, preferred_element_type=jnp.float32),
            ],
            axis=1,
        ),
        "gy",
        scatter_dimension=0,
        tiled=True,
    )
    local_activation = (jax.nn.silu(summed[:, :hidden_width]) * summed[:, hidden_width:]).astype(
        jnp.bfloat16
    )
    activation = lax.all_gather(local_activation, "gy", axis=0, tiled=True)
    row_slab = activation
    down_sum = lax.psum_scatter(
        jnp.dot(row_slab, w_down, preferred_element_type=jnp.float32),
        "gx",
        scatter_dimension=0,
        tiled=True,
    )
    after_mlp = (after_attention.astype(jnp.float32) + down_sum).astype(jnp.bfloat16)
    final_tokens = normalize_rows(after_mlp.astype(jnp.float32), final_gain)
    row_slab = final_tokens
    logits = lax.psum_scatter(
        jnp.dot(row_slab, w_head, preferred_element_type=jnp.float32),
        "gy",
        scatter_dimension=0,
        tiled=True,
    )
    vocab_local = logits.shape[1]
    vocab_start = lax.axis_index("gx") * vocab_local
    chosen = jnp.arange(vocab_local, dtype=jnp.int32)[None, :] + vocab_start == draft_ids[:, None]
    picked_local = jnp.sum(jnp.where(chosen, logits, 0.0), axis=1)
    local_top = jnp.max(logits, axis=1)
    local_sum = jnp.sum(jnp.exp(logits - local_top[:, None]), axis=1)
    highest, exp_total, picked = combined_all(
        (local_top, local_sum, picked_local), "gx", combine_totals
    )
    normalizer = highest + jnp.log(exp_total)
    return (logits - normalizer[:, None], picked - normalizer)


def solution(mesh):
    return jax.shard_map(
        shards,
        mesh=mesh,
        in_specs=(
            P("gx", "gy"),
            P("gy"),
            P("gy"),
            P("gy"),
            P("gy", "gx"),
            P("gy", "gx"),
            P("gy", "gx"),
            P("gx", "gy"),
            P("gy", "gx", None, None),
            P("gy", "gx", None, None),
            P("gy"),
            P("gy", "gx"),
            P("gy", "gx"),
            P("gx", "gy"),
            P("gy"),
            P("gy", "gx"),
        ),
        out_specs=(P("gy", "gx"), P("gy")),
        check_vma=False,
    )
```

profile of v0, /device:TPU:0, one launch (start us, length us, event | category | flops | bytes accessed | tf_op | source)
XLA Modules:
  0.0 791.5 jit_solution(4075788909980705325)
XLA Ops:
  7.2 0.8 convert_element_type.67
  8.0 1.0 fusion.33
  9.0 23.1 %psum.21 = f32[64]{0:T(128)S(1)} all-reduce(f32[64]{0:T(128)S(1)} %fusion.33), channel_id=1, replica_groups=mesh['gx'=4,'gy'=8] {'gy'}, use_global_device_ids=true, to_apply=%region_1.0 | all-reduce | flops 64 | bytes 512 | tf_op jit(solution)/shard_map/psum | solution.py:41
  32.2 1.0 fusion.35
  33.2 7.2 all_gather.33
  40.4 3.5 fusion.55
  43.9 0.3 fusion.56
  44.2 0.3 fusion.57
  44.5 1.8 pad_maximum_fusion.1
  46.6 67.2 %reduce-scatter.6.cloned.1.call-done = f32[32,2560]{1,0:T(8,128)} async-done(((f32[256,2560]{1,0:T(8,128)}), f32[32,2560]{1,0:T(8,128)}) %reduce-scatter.6.cloned.1.call-update) | async-done | bytes 327696 | tf_op jit(solution)/shard_map/reduce_scatter | solution.py:98
  113.8 1.0 slice_bitcast_fusion
  114.9 0.8 slice.55
  116.4 5.1 fusion.54
  121.7 0.3 fusion.27
  122.3 0.8 copy_bitcast_fusion.1
  123.1 4.0 fusion.23
  127.2 0.7 copy.91
  127.9 39.5 %all-gather.6.cloned.1.call-done = bf16[256,2048]{1,0:T(8,128)(2,1)} async-done(((bf16[32,2048]{1,0:T(8,128)(2,1)}), bf16[256,2048]{1,0:T(8,128)(2,1)}) %all-gather.6.cloned.1.call-update) | async-done | bytes 1048592 | tf_op jit(solution)/shard_map/all_gather | solution.py:134
  167.4 4.8 fusion.58
  172.3 23.6 %reduce-scatter.8.cloned.1.call-done = f32[64,1024]{1,0:T(8,128)} async-done(((f32[256,1024]{1,0:T(8,128)}), f32[64,1024]{1,0:T(8,128)}) %reduce-scatter.8.cloned.1.call-update) | async-done | bytes 262160 | tf_op jit(solution)/shard_map/reduce_scatter | solution.py:136
  195.9 1.1 fusion.37
  197.0 21.4 %psum.22 = f32[64]{0:T(128)S(1)} all-reduce(f32[64]{0:T(128)S(1)} %get-tuple-element.206), channel_id=1, replica_groups=mesh['gx'=4,'gy'=8] {'gy'}, use_global_device_ids=true, to_apply=%region_7.8 | all-reduce | flops 64 | bytes 512 | tf_op jit(solution)/shard_map/psum | solution.py:41
  218.5 6.7 all_gather.35
  225.2 7.4 fusion.59
  232.6 0.2 slice-done.2
  232.8 1.2 slice-done.3
  234.0 4.1 fusion.60
  238.1 5.5 pad_maximum_fusion
  243.6 233.7 %reduce-scatter.10.cloned.1.call-done = f32[32,14336]{1,0:T(8,128)} async-done(((f32[256,14336]{1,0:T(8,128)}), f32[32,14336]{1,0:T(8,128)}) %reduce-scatter.10.cloned.1.call-update) | async-done | bytes 1835024 | tf_op jit(solution)/shard_map/reduce_scatter | solution.py:146
  477.4 2.5 fusion.26
  479.9 65.4 %all-gather.8.cloned.1.call-done = bf16[256,7168]{1,0:T(8,128)(2,1)} async-done(((bf16[32,7168]{1,0:T(8,128)(2,1)}), bf16[256,7168]{1,0:T(8,128)(2,1)}) %all-gather.8.cloned.1.call-update) | async-done | bytes 3670032 | tf_op jit(solution)/shard_map/all_gather | solution.py:161
  545.3 11.2 %fusion.61 = f32[256,1024]{1,0:T(8,128)} fusion(bf16[256,7168]{1,0:T(8,128)(2,1)} %all-gather.8.cloned.1.call-done, bf16[7168,1024]{1,0:T(8,128)(2,1)} %param.31), kind=kOutput, calls=%fused_computation.92 | convolution fusion | flops 3758096384 | bytes 19398656 | tf_op jit(solution)/shard_map/dot_general | solution.py:164
  556.6 23.6 %reduce-scatter.12.cloned.1.call-done = f32[64,1024]{1,0:T(8,128)} async-done(((f32[256,1024]{1,0:T(8,128)}), f32[64,1024]{1,0:T(8,128)}) %reduce-scatter.12.cloned.1.call-update) | async-done | bytes 262160 | tf_op jit(solution)/shard_map/reduce_scatter | solution.py:163
  580.2 1.1 fusion.30
  581.3 21.4 %psum.23 = f32[64]{0:T(128)S(1)} all-reduce(f32[64]{0:T(128)S(1)} %fusion.30), channel_id=1, replica_groups=mesh['gx'=4,'gy'=8] {'gy'}, use_global_device_ids=true, to_apply=%region_11.12 | all-reduce | flops 64 | bytes 512 | tf_op jit(solution)/shard_map/psum | solution.py:41
  602.7 1.0 fusion.32
  603.8 6.7 all_gather.37
  610.5 18.4 %fusion.62 = f32[256,8000]{1,0:T(8,128)} fusion(bf16[256,1024]{1,0:T(8,128)(2,1)S(1)} %all_gather.37, bf16[1024,8000]{0,1:T(8,128)(2,1)} %param.33), kind=kOutput, calls=%fused_computation.93 | convolution fusion | flops 4194304000 | bytes 25100288 | tf_op jit(solution)/shard_map/dot_general | solution.py:173
  629.0 0.6 copy-done.8
  629.6 0.6 dynamic-slice
  630.8 141.3 %reduce-scatter.14.cloned.1.call-done = f32[32,8000]{1,0:T(8,128)} async-done(((f32[256,8000]{1,0:T(8,128)}), f32[32,8000]{1,0:T(8,128)}) %reduce-scatter.14.cloned.1.call-update) | async-done | bytes 1024016 | tf_op jit(solution)/shard_map/reduce_scatter | solution.py:172
  772.1 1.4 reduce_max.22
  773.5 0.2 dynamic-update-slice
  773.7 1.6 select_reduce_fusion
  775.4 0.2 dynamic-update-slice.2
  775.8 5.6 all-reduce.3
  781.8 0.5 fusion.52
  782.3 2.3 broadcast_subtract_fusion
  (77 shorter events, 2.7 us)
Async XLA Ops:
  7.2 36.7 %copy-start = (bf16[1024,256]{1,0:T(8,128)(2,1)S(1)}, bf16[1024,256]{1,0:T(8,128)(2,1)}, u32[]{:S(2)}) copy-start(bf16[1024,256]{1,0:T(8,128)(2,1)} %param.23) | copy-start | bytes 1572868
  7.2 37.0 %copy-start.3 = (bf16[1024,256]{1,0:T(8,128)(2,1)S(1)}, bf16[1024,256]{1,0:T(8,128)(2,1)}, u32[]{:S(2)}) copy-start(bf16[1024,256]{1,0:T(8,128)(2,1)} %param.24) | copy-start | bytes 1572868
  7.2 106.6 %reduce-scatter.6.cloned.1.call-start = ((), (), s32[]{:S(2)}) async-start(), calls=%async_computation.5 | async-start | bytes 2949120 | tf_op jit(solution)/shard_map/reduce_scatter | solution.py:98
  43.9 2.5 copy-start.7
  46.3 121.2 %all-gather.6.cloned.1.call-start = ((), (), s32[]{:S(2)}) async-start(), calls=%async_computation.6 | async-start | bytes 1179648 | tf_op jit(solution)/shard_map/all_gather | solution.py:134
  127.1 45.2 %copy-start.4 = (bf16[1024]{0:T(1024)(128)(2,1)S(1)}, bf16[1024]{0:T(1024)(128)(2,1)}, u32[]{:S(2)}) copy-start(bf16[1024]{0:T(1024)(128)(2,1)} %param.28) | copy-start | bytes 6148
  127.1 68.8 %copy-start.2 = (bf16[64,1024]{1,0:T(8,128)(2,1)S(1)}, bf16[64,1024]{1,0:T(8,128)(2,1)}, u32[]{:S(2)}) copy-start(bf16[64,1024]{1,0:T(8,128)(2,1)} %param.18) | copy-start | bytes 393220
  127.9 68.0 %reduce-scatter.8.cloned.1.call-start = ((), (), s32[]{:S(2)}) async-start(), calls=%async_computation.7 | async-start | bytes 1310720 | tf_op jit(solution)/shard_map/reduce_scatter | solution.py:136
  172.2 60.4 %slice-start = ((s8[14680064]{0:T(1024)(128)(4,1)}), s8[2097152]{0:T(1024)(128)(4,1)S(1)}, s32[]{:S(2)}) async-start(s8[14680064]{0:T(1024)(128)(4,1)} %bitcast.94), calls=%async_computation.12 | async-start | bytes 4194304
  172.2 305.1 %reduce-scatter.10.cloned.1.call-start = ((), (), s32[]{:S(2)}) async-start(), calls=%async_computation.8 | async-start | bytes 16515072 | tf_op jit(solution)/shard_map/reduce_scatter | solution.py:146
  225.2 7.4 slice-start.1
  225.2 7.6 slice-start.2
  225.2 8.8 %slice-start.3 = ((s8[14680064]{0:T(1024)(128)(4,1)}), s8[4194304]{0:T(1024)(128)(4,1)S(1)}, s32[]{:S(2)}) async-start(s8[14680064]{0:T(1024)(128)(4,1)} %bitcast.94), calls=%async_computation.15 | async-start | bytes 8388608
  243.6 301.8 %all-gather.8.cloned.1.call-start = ((), (), s32[]{:S(2)}) async-start(), calls=%async_computation.9 | async-start | bytes 4128768 | tf_op jit(solution)/shard_map/all_gather | solution.py:161
  479.9 76.7 %copy-start.5 = (bf16[1024]{0:T(1024)(128)(2,1)S(1)}, bf16[1024]{0:T(1024)(128)(2,1)}, u32[]{:S(2)}) copy-start(bf16[1024]{0:T(1024)(128)(2,1)} %param.32) | copy-start | bytes 6148
  479.9 100.3 %reduce-scatter.12.cloned.1.call-start = ((), (), s32[]{:S(2)}) async-start(), calls=%async_computation.10 | async-start | bytes 1310720 | tf_op jit(solution)/shard_map/reduce_scatter | solution.py:163
  556.6 215.5 %reduce-scatter.14.cloned.1.call-start = ((), (), s32[]{:S(2)}) async-start(), calls=%async_computation.11 | async-start | bytes 9289728 | tf_op jit(solution)/shard_map/reduce_scatter | solution.py:172
  628.9 0.7 copy-start.8
  628.9 144.8 %copy-start.6 = (s32[32]{0:T(128)S(1)}, s32[32]{0:T(128)}, u32[]{:S(2)}) copy-start(s32[32]{0:T(128)} %param.20) | copy-start | bytes 388
  628.9 155.7 %copy-start.1 = (bf16[1024,256]{1,0:T(8,128)(2,1)S(1)}, bf16[1024,256]{1,0:T(8,128)(2,1)}, u32[]{:S(2)}) copy-start(bf16[1024,256]{1,0:T(8,128)(2,1)} %param.23) | copy-start | bytes 1572868
Sparse Core Ops, SparseCore 0:
  46.4 67.3 reduce-scatter.5
  128.0 39.4 all-gather.5
  172.3 23.4 reduce-scatter.7
  243.7 233.6 reduce-scatter.9
  480.0 65.3 all-gather.7
  556.7 23.4 reduce-scatter.11
  629.1 142.9 reduce-scatter.13
where the time goes:
time: 792 us
  waiting for transfers between devices  594 us (75%)
  blocking collectives  92.1 us (12%)
  matrix products  59.3 us (7%)
  other arithmetic  23.6 us (3%)
  between operations  15.1 us (2%)
    reduce_scatter x1, waiting for transfers between devices, shards(): lax.psum_scatter(jnp.concatenate([jnp.dot(row_slab, w_gate, preferred_ele...  234 us
    reduce_scatter x1, waiting for transfers between devices, shards(): lax.psum_scatter(jnp.dot(row_slab, w_head, preferred_element_type=jnp.flo...  141 us
    reduce_scatter x1, waiting for transfers between devices, shards(): lax.psum_scatter(jnp.concatenate([jnp.dot(row_slab, w_query, preferred_el...  67.2 us
    psum x3, blocking collectives, normalize_rows(): squares = lax.psum(jnp.sum(activity * activity, axis=1), 'gy')  65.9 us
    all_gather x1, waiting for transfers between devices, shards(): activation = lax.all_gather(local_activation, 'gy', axis=0, tiled=True)  65.4 us
    all_gather x1, waiting for transfers between devices, shards(): all_heads = lax.all_gather(attended, 'gy', axis=0, tiled=True)  39.5 us
    reduce_scatter x1, waiting for transfers between devices, shards(): lax.psum_scatter(jnp.dot(row_slab, w_down, preferred_element_type=jnp.flo...  23.6 us
    reduce_scatter x1, waiting for transfers between devices, shards(): lax.psum_scatter(jnp.dot(row_slab, w_out, preferred_element_type=jnp.floa...  23.6 us
  transfers between devices with their start and end apart: 7, of which 7 were waited for; matrix products, arithmetic and copies ran while one was open for 0% of the time, Pallas kernels for 0%

commit v1 on v0

--- a/solution.py
+++ b/solution.py
@@ -6,6 +6,17 @@
 D = 8192
 HEAD_DIM = 128
 epsilon = 1e-05
+
+
+def turned_line(x, mesh_axis, dim):
+    peers = lax.axis_size(mesh_axis)
+    hops = [(i, (i + 1) % peers) for i in range(peers)]
+    terms = [x]
+    for stride in range(1, peers):
+        terms = [lax.ppermute(terms[0], mesh_axis, hops), *terms]
+    whole = jnp.concatenate(terms, axis=dim)
+    shift = (lax.axis_index(mesh_axis) + 1) * terms[-1].shape[dim]
+    return jnp.roll(whole, shift, axis=dim)
 
 
 def combined_all(x, axis, combine):
@@ -158,7 +169,7 @@
     local_activation = (jax.nn.silu(summed[:, :hidden_width]) * summed[:, hidden_width:]).astype(
         jnp.bfloat16
     )
-    activation = lax.all_gather(local_activation, "gy", axis=0, tiled=True)
+    activation = turned_line(local_activation, "gy", 0)
     row_slab = activation
     down_sum = lax.psum_scatter(
         jnp.dot(row_slab, w_down, preferred_element_type=jnp.float32),

time: 792 us -> 819 us (1.034)
  waiting for transfers between devices: 594 us -> 614 us
    ppermute x0 -> x7, waiting for transfers between devices: none -> 87.3 us  [turned_line(): terms = [lax.ppermute(terms[0], mesh_axis, hops), *terms]]
    all_gather x1 -> x0, waiting for transfers between devices: 65.4 us -> none  [shards(): activation = lax.all_gather(local_activation, 'gy', axis=0, tiled=True)]
  transfers between devices with their start and end apart: 7 -> 13, of which waited for: 7 -> 13; matrix products, arithmetic and copies ran while one was open for 0% -> 0% of each run, Pallas kernels for 0% -> 0%
where the time goes in v1:
time: 819 us; the launch traced here: 818 us
  waiting for transfers between devices  614 us (75%)
  blocking collectives  92.1 us (11%)
  matrix products  56.5 us (7%)
  other arithmetic  23.5 us (3%)
  between operations  15.2 us (2%)
  local copies, waits for them, and re-layouts  14.7 us (2%)
    reduce_scatter x1, waiting for transfers between devices, shards(): lax.psum_scatter(jnp.concatenate([jnp.dot(row_slab, w_gate, preferred_ele...  234 us
    reduce_scatter x1, waiting for transfers between devices, shards(): lax.psum_scatter(jnp.dot(row_slab, w_head, preferred_element_type=jnp.flo...  141 us
    ppermute x7, waiting for transfers between devices, turned_line(): terms = [lax.ppermute(terms[0], mesh_axis, hops), *terms]  87.3 us
    reduce_scatter x1, waiting for transfers between devices, shards(): lax.psum_scatter(jnp.concatenate([jnp.dot(row_slab, w_query, preferred_el...  67.3 us
    psum x3, blocking collectives, normalize_rows(): squares = lax.psum(jnp.sum(activity * activity, axis=1), 'gy')  65.9 us
    all_gather x1, waiting for transfers between devices, shards(): all_heads = lax.all_gather(attended, 'gy', axis=0, tiled=True)  39.5 us
    reduce_scatter x1, waiting for transfers between devices, shards(): lax.psum_scatter(jnp.dot(row_slab, w_out, preferred_element_type=jnp.floa...  23.6 us
    reduce_scatter x1, waiting for transfers between devices, shards(): lax.psum_scatter(jnp.dot(row_slab, w_down, preferred_element_type=jnp.flo...  22 us
  transfers between devices with their start and end apart: 13, of which 13 were waited for; matrix products, arithmetic and copies ran while one was open for 0% of the time, Pallas kernels for 0%

profile of v1, /device:TPU:0, one launch (start us, length us, event | category | flops | bytes accessed | tf_op | source)
XLA Modules:
  0.0 818.3 jit_solution(15705087490672321216)
XLA Ops:
  8.0 1.0 fusion.35
  9.0 23.1 %psum.21 = f32[64]{0:T(128)S(1)} all-reduce(f32[64]{0:T(128)S(1)} %fusion.35), channel_id=1, replica_groups=mesh['gx'=4,'gy'=8] {'gy'}, use_global_device_ids=true, to_apply=%region_1.0 | all-reduce | flops 64 | bytes 512 | tf_op jit(solution)/shard_map/psum | solution.py:52
  32.2 1.0 fusion.37
  33.2 7.2 all_gather.30
  40.4 3.5 fusion.58
  44.5 1.8 pad_maximum_fusion.1
  46.6 67.3 %reduce-scatter.6.cloned.1.call-done = f32[32,2560]{1,0:T(8,128)} async-done(((f32[256,2560]{1,0:T(8,128)}), f32[32,2560]{1,0:T(8,128)}) %reduce-scatter.6.cloned.1.call-update) | async-done | bytes 327696 | tf_op jit(solution)/shard_map/reduce_scatter | solution.py:109
  113.9 1.0 slice_bitcast_fusion
  116.5 5.1 fusion.57
  123.1 4.1 fusion.25
  128.0 39.5 %all-gather.5.cloned.1.call-done = bf16[256,2048]{1,0:T(8,128)(2,1)} async-done(((bf16[32,2048]{1,0:T(8,128)(2,1)}), bf16[256,2048]{1,0:T(8,128)(2,1)}) %all-gather.5.cloned.1.call-update) | async-done | bytes 1048592 | tf_op jit(solution)/shard_map/all_gather | solution.py:145
  167.5 4.7 fusion.61
  172.3 23.6 %reduce-scatter.8.cloned.1.call-done = f32[64,1024]{1,0:T(8,128)} async-done(((f32[256,1024]{1,0:T(8,128)}), f32[64,1024]{1,0:T(8,128)}) %reduce-scatter.8.cloned.1.call-update) | async-done | bytes 262160 | tf_op jit(solution)/shard_map/reduce_scatter | solution.py:147
  195.9 1.1 fusion.39
  197.0 21.4 %psum.22 = f32[64]{0:T(128)S(1)} all-reduce(f32[64]{0:T(128)S(1)} %get-tuple-element.206), channel_id=1, replica_groups=mesh['gx'=4,'gy'=8] {'gy'}, use_global_device_ids=true, to_apply=%region_7.8 | all-reduce | flops 64 | bytes 512 | tf_op jit(solution)/shard_map/psum | solution.py:52
  218.5 6.7 all_gather.32
  225.2 7.4 fusion.62
  232.8 1.2 slice-done.3
  234.0 4.1 fusion.63
  238.1 5.5 pad_maximum_fusion
  243.6 233.8 %reduce-scatter.10.cloned.1.call-done = f32[32,14336]{1,0:T(8,128)} async-done(((f32[256,14336]{1,0:T(8,128)}), f32[32,14336]{1,0:T(8,128)}) %reduce-scatter.10.cloned.1.call-update) | async-done | bytes 1835024 | tf_op jit(solution)/shard_map/reduce_scatter | solution.py:157
  477.4 1.8 fusion.28
  479.2 1.5 collective-permute-start
  480.8 13.4 %collective-permute-done = bf16[32,7168]{1,0:T(8,128)(2,1)S(1)} collective-permute-done((bf16[32,7168]{1,0:T(8,128)(2,1)S(1)}, bf16[32,7168]{1,0:T(8,128)(2,1)S(1)}, u32[]{:S(2)}, u32[]{:S(2)}) %collective-permute-start) | collective-permute-done | bytes 458784 | tf_op jit(solution)/shard_map/ppermute | solution.py:16
  494.2 14.0 %collective-permute-done.1 = bf16[32,7168]{1,0:T(8,128)(2,1)S(1)} collective-permute-done((bf16[32,7168]{1,0:T(8,128)(2,1)S(1)}, bf16[32,7168]{1,0:T(8,128)(2,1)S(1)}, u32[]{:S(2)}, u32[]{:S(2)}) %collective-permute-start.1) | collective-permute-done | bytes 458784 | tf_op jit(solution)/shard_map/ppermute | solution.py:16
  508.2 13.2 %collective-permute-done.2 = bf16[32,7168]{1,0:T(8,128)(2,1)S(1)} collective-permute-done((bf16[32,7168]{1,0:T(8,128)(2,1)S(1)}, bf16[32,7168]{1,0:T(8,128)(2,1)S(1)}, u32[]{:S(2)}, u32[]{:S(2)}) %collective-permute-start.2) | collective-permute-done | bytes 458784 | tf_op jit(solution)/shard_map/ppermute | solution.py:16
  521.4 12.3 %collective-permute-done.3 = bf16[32,7168]{1,0:T(8,128)(2,1)S(1)} collective-permute-done((bf16[32,7168]{1,0:T(8,128)(2,1)S(1)}, bf16[32,7168]{1,0:T(8,128)(2,1)S(1)}, u32[]{:S(2)}, u32[]{:S(2)}) %collective-permute-start.3) | collective-permute-done | bytes 458784 | tf_op jit(solution)/shard_map/ppermute | solution.py:16
  534.6 11.5 %collective-permute-done.4 = bf16[32,7168]{1,0:T(8,128)(2,1)S(1)} collective-permute-done((bf16[32,7168]{1,0:T(8,128)(2,1)S(1)}, bf16[32,7168]{1,0:T(8,128)(2,1)S(1)}, u32[]{:S(2)}, u32[]{:S(2)}) %collective-permute-start.4) | collective-permute-done | bytes 458784 | tf_op jit(solution)/shard_map/ppermute | solution.py:16
  546.8 11.3 %collective-permute-done.5 = bf16[32,7168]{1,0:T(8,128)(2,1)} collective-permute-done((bf16[32,7168]{1,0:T(8,128)(2,1)S(1)}, bf16[32,7168]{1,0:T(8,128)(2,1)}, u32[]{:S(2)}, u32[]{:S(2)}) %collective-permute-start.5) | collective-permute-done | bytes 458784 | tf_op jit(solution)/shard_map/ppermute | solution.py:16
  558.1 11.5 %collective-permute-done.6 = bf16[32,7168]{1,0:T(8,128)(2,1)} collective-permute-done((bf16[32,7168]{1,0:T(8,128)(2,1)}, bf16[32,7168]{1,0:T(8,128)(2,1)}, u32[]{:S(2)}, u32[]{:S(2)}) %collective-permute-start.6) | collective-permute-done | bytes 458784 | tf_op jit(solution)/shard_map/ppermute | solution.py:16
  569.6 1.0 constant_dynamic-update-slice_fusion.15
  570.7 1.1 constant_dynamic-update-slice_fusion.14
  571.7 1.1 constant_dynamic-update-slice_fusion.13
  572.8 1.1 constant_dynamic-update-slice_fusion.12
  574.2 1.1 constant_dynamic-update-slice_fusion.7
  575.3 1.1 constant_dynamic-update-slice_fusion.6
  576.8 8.3 %fusion.11 = f32[256,1024]{1,0:T(8,128)} fusion(bf16[7168,1024]{1,0:T(8,128)(2,1)} %param.31, bf16[512,7168]{1,0:T(8,128)(2,1)S(1)} %constant_dynamic-update-slice_fusion, s32[]{:T(128)S(6)} %select_n.35), kind=kOutput, calls=%fused_computation.15 | convolution fusion | flops 3758096384 | bytes 19398660 | tf_op jit(solution)/shard_map/dot_general | solution.py:175
  585.2 22.0 %reduce-scatter.12.cloned.1.call-done = f32[64,1024]{1,0:T(8,128)} async-done(((f32[256,1024]{1,0:T(8,128)}), f32[64,1024]{1,0:T(8,128)}) %reduce-scatter.12.cloned.1.call-update) | async-done | bytes 262160 | tf_op jit(solution)/shard_map/reduce_scatter | solution.py:174
  607.3 1.1 fusion.32
  608.4 21.4 %psum.23 = f32[64]{0:T(128)S(1)} all-reduce(f32[64]{0:T(128)S(1)} %fusion.32), channel_id=1, replica_groups=mesh['gx'=4,'gy'=8] {'gy'}, use_global_device_ids=true, to_apply=%region_11.12 | all-reduce | flops 64 | bytes 512 | tf_op jit(solution)/shard_map/psum | solution.py:52
  629.7 1.0 fusion.34
  630.8 6.7 all_gather.33
  637.5 18.5 %fusion.64 = f32[256,8000]{1,0:T(8,128)} fusion(bf16[256,1024]{1,0:T(8,128)(2,1)S(1)} %all_gather.33, bf16[1024,8000]{0,1:T(8,128)(2,1)} %param.33), kind=kOutput, calls=%fused_computation.111 | convolution fusion | flops 4194304000 | bytes 25100288 | tf_op jit(solution)/shard_map/dot_general | solution.py:184
  657.9 140.9 %reduce-scatter.14.cloned.1.call-done = f32[32,8000]{1,0:T(8,128)} async-done(((f32[256,8000]{1,0:T(8,128)}), f32[32,8000]{1,0:T(8,128)}) %reduce-scatter.14.cloned.1.call-update) | async-done | bytes 1024016 | tf_op jit(solution)/shard_map/reduce_scatter | solution.py:183
  798.9 1.4 reduce_max.22
  800.5 1.6 select_reduce_fusion
  802.6 5.6 all-reduce.3
  809.1 2.3 broadcast_subtract_fusion
  (114 shorter events, 11.3 us)
Async XLA Ops:
  7.2 36.7 %copy-start = (bf16[1024,256]{1,0:T(8,128)(2,1)S(1)}, bf16[1024,256]{1,0:T(8,128)(2,1)}, u32[]{:S(2)}) copy-start(bf16[1024,256]{1,0:T(8,128)(2,1)} %param.23) | copy-start | bytes 1572868
  7.2 37.0 %copy-start.8 = (bf16[1024,256]{1,0:T(8,128)(2,1)S(1)}, bf16[1024,256]{1,0:T(8,128)(2,1)}, u32[]{:S(2)}) copy-start(bf16[1024,256]{1,0:T(8,128)(2,1)} %param.24) | copy-start | bytes 1572868
  7.2 106.7 %reduce-scatter.6.cloned.1.call-start = ((), (), s32[]{:S(2)}) async-start(), calls=%async_computation.5 | async-start | bytes 2949120 | tf_op jit(solution)/shard_map/reduce_scatter | solution.py:109
  40.4 6.0 copy-start.12
  46.3 121.2 %all-gather.5.cloned.1.call-start = ((), (), s32[]{:S(2)}) async-start(), calls=%async_computation.6 | async-start | bytes 1179648 | tf_op jit(solution)/shard_map/all_gather | solution.py:145
  123.1 49.2 %copy-start.9 = (bf16[1024]{0:T(1024)(128)(2,1)S(1)}, bf16[1024]{0:T(1024)(128)(2,1)}, u32[]{:S(2)}) copy-start(bf16[1024]{0:T(1024)(128)(2,1)} %param.28) | copy-start | bytes 6148
  123.1 72.8 %copy-start.7 = (bf16[64,1024]{1,0:T(8,128)(2,1)S(1)}, bf16[64,1024]{1,0:T(8,128)(2,1)}, u32[]{:S(2)}) copy-start(bf16[64,1024]{1,0:T(8,128)(2,1)} %param.18) | copy-start | bytes 393220
  127.9 68.0 %reduce-scatter.8.cloned.1.call-start = ((), (), s32[]{:S(2)}) async-start(), calls=%async_computation.7 | async-start | bytes 1310720 | tf_op jit(solution)/shard_map/reduce_scatter | solution.py:147
  172.2 60.4 %slice-start = ((s8[14680064]{0:T(1024)(128)(4,1)}), s8[2097152]{0:T(1024)(128)(4,1)S(1)}, s32[]{:S(2)}) async-start(s8[14680064]{0:T(1024)(128)(4,1)} %bitcast.93), calls=%async_computation.11 | async-start | bytes 4194304
  172.2 305.1 %reduce-scatter.10.cloned.1.call-start = ((), (), s32[]{:S(2)}) async-start(), calls=%async_computation.8 | async-start | bytes 16515072 | tf_op jit(solution)/shard_map/reduce_scatter | solution.py:157
  225.2 7.4 slice-start.1
  225.2 7.6 slice-start.2
  225.2 8.8 %slice-start.3 = ((s8[14680064]{0:T(1024)(128)(4,1)}), s8[4194304]{0:T(1024)(128)(4,1)S(1)}, s32[]{:S(2)}) async-start(s8[14680064]{0:T(1024)(128)(4,1)} %bitcast.93), calls=%async_computation.14 | async-start | bytes 8388608
  243.6 363.7 %reduce-scatter.12.cloned.1.call-start = ((), (), s32[]{:S(2)}) async-start(), calls=%async_computation.9 | async-start | bytes 1310720 | tf_op jit(solution)/shard_map/reduce_scatter | solution.py:174
  477.4 96.6 %copy-start.2 = (f32[32,14336]{1,0:T(8,128)S(1)}, f32[32,14336]{1,0:T(8,128)}, u32[]{:S(2)}) copy-start(f32[32,14336]{1,0:T(8,128)} %reduce-scatter.10.cloned.1.call-done) | copy-start | bytes 5505028
  479.2 15.0 %collective-permute-start = (bf16[32,7168]{1,0:T(8,128)(2,1)S(1)}, bf16[32,7168]{1,0:T(8,128)(2,1)S(1)}, u32[]{:S(2)}, u32[]{:S(2)}) collective-permute-start(bf16[32,7168]{1,0:T(8,128)(2,1)S(1)} %fusion.28), channel_id=1, source_target_pairs={{0,1},{1,2},{2,3},{3,4},{4,5},{5,6},{6,7},{7,0},{8,9},{9,10},{10,1... | collective-permute-start | bytes 1376264 | tf_op jit(solution)/shard_map/ppermute | solution.py:16
  494.2 14.1 %collective-permute-start.1 = (bf16[32,7168]{1,0:T(8,128)(2,1)S(1)}, bf16[32,7168]{1,0:T(8,128)(2,1)S(1)}, u32[]{:S(2)}, u32[]{:S(2)}) collective-permute-start(bf16[32,7168]{1,0:T(8,128)(2,1)S(1)} %collective-permute-done), channel_id=1, source_target_pairs={{0,1},{1,2},{2,3},{3,4},{4,5},{5,6},{6,7},{7,0},{8,9},{9,10},{10,1... | collective-permute-start | bytes 1376264 | tf_op jit(solution)/shard_map/ppermute | solution.py:16
  508.2 13.2 %collective-permute-start.2 = (bf16[32,7168]{1,0:T(8,128)(2,1)S(1)}, bf16[32,7168]{1,0:T(8,128)(2,1)S(1)}, u32[]{:S(2)}, u32[]{:S(2)}) collective-permute-start(bf16[32,7168]{1,0:T(8,128)(2,1)S(1)} %collective-permute-done.1), channel_id=1, source_target_pairs={{0,1},{1,2},{2,3},{3,4},{4,5},{5,6},{6,7},{7,0},{8,9},{9,10},{10,1... | collective-permute-start | bytes 1376264 | tf_op jit(solution)/shard_map/ppermute | solution.py:16
  521.4 12.3 %collective-permute-start.3 = (bf16[32,7168]{1,0:T(8,128)(2,1)S(1)}, bf16[32,7168]{1,0:T(8,128)(2,1)S(1)}, u32[]{:S(2)}, u32[]{:S(2)}) collective-permute-start(bf16[32,7168]{1,0:T(8,128)(2,1)S(1)} %collective-permute-done.2), channel_id=1, source_target_pairs={{0,1},{1,2},{2,3},{3,4},{4,5},{5,6},{6,7},{7,0},{8,9},{9,10},{10,1... | collective-permute-start | bytes 1376264 | tf_op jit(solution)/shard_map/ppermute | solution.py:16
  533.8 0.8 copy-start.3
  534.6 11.5 %collective-permute-start.4 = (bf16[32,7168]{1,0:T(8,128)(2,1)S(1)}, bf16[32,7168]{1,0:T(8,128)(2,1)S(1)}, u32[]{:S(2)}, u32[]{:S(2)}) collective-permute-start(bf16[32,7168]{1,0:T(8,128)(2,1)S(1)} %collective-permute-done.3), channel_id=1, source_target_pairs={{0,1},{1,2},{2,3},{3,4},{4,5},{5,6},{6,7},{7,0},{8,9},{9,10},{10,1... | collective-permute-start | bytes 1376264 | tf_op jit(solution)/shard_map/ppermute | solution.py:16
  546.0 0.8 copy-start.5
  546.8 11.3 %collective-permute-start.5 = (bf16[32,7168]{1,0:T(8,128)(2,1)S(1)}, bf16[32,7168]{1,0:T(8,128)(2,1)}, u32[]{:S(2)}, u32[]{:S(2)}) collective-permute-start(bf16[32,7168]{1,0:T(8,128)(2,1)S(1)} %collective-permute-done.4), channel_id=1, source_target_pairs={{0,1},{1,2},{2,3},{3,4},{4,5},{5,6},{6,7},{7,0},{8,9},{9,10},{10,1... | collective-permute-start | bytes 1376264 | tf_op jit(solution)/shard_map/ppermute | solution.py:16
  558.1 11.5 %collective-permute-start.6 = (bf16[32,7168]{1,0:T(8,128)(2,1)}, bf16[32,7168]{1,0:T(8,128)(2,1)}, u32[]{:S(2)}, u32[]{:S(2)}) collective-permute-start(bf16[32,7168]{1,0:T(8,128)(2,1)} %collective-permute-done.5), channel_id=1, source_target_pairs={{0,1},{1,2},{2,3},{3,4},{4,5},{5,6},{6,7},{7,0},{8,9},{9,10},{10,1... | collective-permute-start | bytes 1376264 | tf_op jit(solution)/shard_map/ppermute | solution.py:16
  558.1 18.2 %copy-start.6 = (bf16[32,7168]{1,0:T(8,128)(2,1)S(1)}, bf16[32,7168]{1,0:T(8,128)(2,1)}, u32[]{:S(2)}) copy-start(bf16[32,7168]{1,0:T(8,128)(2,1)} %copy-done.5) | copy-start | bytes 1376260
  558.1 18.2 %copy-start.4 = (bf16[32,7168]{1,0:T(8,128)(2,1)S(1)}, bf16[32,7168]{1,0:T(8,128)(2,1)}, u32[]{:S(2)}) copy-start(bf16[32,7168]{1,0:T(8,128)(2,1)} %copy-done.3) | copy-start | bytes 1376260
  576.8 8.4 %copy-start.10 = (bf16[1024]{0:T(1024)(128)(2,1)S(1)}, bf16[1024]{0:T(1024)(128)(2,1)}, u32[]{:S(2)}) copy-start(bf16[1024]{0:T(1024)(128)(2,1)} %param.32) | copy-start | bytes 6148
  585.1 213.7 %reduce-scatter.14.cloned.1.call-start = ((), (), s32[]{:S(2)}) async-start(), calls=%async_computation.10 | async-start | bytes 9289728 | tf_op jit(solution)/shard_map/reduce_scatter | solution.py:183
  637.5 173.9 %copy-start.1 = (bf16[1024,256]{1,0:T(8,128)(2,1)S(1)}, bf16[1024,256]{1,0:T(8,128)(2,1)}, u32[]{:S(2)}) copy-start(bf16[1024,256]{1,0:T(8,128)(2,1)} %param.23) | copy-start | bytes 1572868
  656.0 0.7 copy-start.13
  656.0 144.5 %copy-start.11 = (s32[32]{0:T(128)S(1)}, s32[32]{0:T(128)}, u32[]{:S(2)}) copy-start(s32[32]{0:T(128)} %param.20) | copy-start | bytes 388
Sparse Core Ops, SparseCore 0:
  46.4 67.3 reduce-scatter.5
  128.1 39.3 all-gather.4
  172.4 23.4 reduce-scatter.7
  243.7 233.6 reduce-scatter.9
  585.3 21.9 reduce-scatter.11
  656.2 142.6 reduce-scatter.13
